TPU v7x, 32 devices: a whole 2x2x4 slice. The times are simulated.
32 devices in a mesh: samp: 8 (over z, core), chan: 4 (over y, x).
Axes of the slice: x: 2, y: 2, z: 4, core: 2. Of those that a mesh axis runs over, the one named last changes fastest.
Arguments:
- out_cot: bfloat16 [8, 256, 4096], P('samp', 'chan'), may hold values from -6 to 6
- mix_weight: bfloat16 [256, 256], replicated, may hold values from -0.375 to 0.375
- corr_kernels: float32 [2, 12, 256, 64], P(None, None, 'chan'), may hold values from -0.75 to 0.75
- momentum: int32 [8], P('samp'), may hold values from 0 to 11
- spin_up: int32 [8, 4096], P('samp', 'chan'), may hold values 0 or 1
- layer_input: bfloat16 [8, 256, 4096], P('samp', None, 'chan'), may hold values from -6 to 6
- pre_one: bfloat16 [8, 256, 4096], P('samp', None, 'chan'), may hold values from -6 to 6
- pre_two: bfloat16 [8, 256, 4096], P('samp', None, 'chan'), may hold values from -6 to 6
- conv_weight: bfloat16 [3, 9, 256, 256], replicated, may hold values from -0.125 to 0.125
- dilation: int32 [3, 256], replicated, may hold values from 1 to 4, as said below
Outputs:
- input_grad: bfloat16 [8, 256, 4096], P('samp', None, 'chan')
- weight_grad: float32 [3, 9, 256, 256], P(None, None, 'chan')
Inputs may be any that keep to these rules, and one draw needn't show every extreme that they name: Some channel of every convolution has dilation 4.
All inputs are finite; a program needn't handle non-finite values. No bound on the sum of `spin_up` on one device may be relied on, other than what follows from the above.
Results may differ from a plain program's by a relative error of at most 0.02.
Values may be sent and summed in bfloat16 or wider, within the bound.
A program may use at most 64 MiB of HBM per device.

v0:
```python
import math
import jax
import jax.numpy as jnp
from jax import lax
from jax.sharding import PartitionSpec as P

SIDE = 64
LAYERS = 3
MAXDIL = 4


def with_halo(shard, sides, width):
    for axis, dim in sides:
        size, length = (lax.axis_size(axis), shard.shape[dim])
        up = [(i, (i + 1) % size) for i in range(size)]
        down = [(j, i) for i, j in up]
        last = lax.slice_in_dim(shard, length - width, length, axis=dim)
        leading = lax.slice_in_dim(shard, 0, width, axis=dim)
        before = lax.ppermute(last, axis, up)
        after = lax.ppermute(leading, axis, down)
        shard = jnp.concatenate([before, shard, after], axis=dim)
    return shard


def column_shift(values, step_size, lattice_side, column):
    if step_size == 0:
        return values
    inside = (column - step_size >= 0) & (column - step_size < lattice_side)
    wrapped = step_size - lattice_side if step_size > 0 else step_size + lattice_side
    return jnp.where(inside, jnp.roll(values, step_size, axis=2), jnp.roll(values, wrapped, axis=2))


def on_device(
    out_cot,
    mix_weight,
    corr_kernels,
    momentum,
    spin_up,
    layer_input,
    pre_one,
    pre_two,
    conv_weight,
    dilation,
):
    highest = lax.Precision.HIGHEST
    sample_count = out_cot.shape[0]
    chan_block = out_cot.shape[1]
    site_count = out_cot.shape[2]
    sectors = corr_kernels.shape[1]
    lattice_side = corr_kernels.shape[3]
    slab_cells = layer_input.shape[2]
    own_start = lax.axis_index("chan") * chan_block
    own_rows = lax.dynamic_slice_in_dim(mix_weight, own_start, chan_block, 0)
    input_cot = lax.psum_scatter(
        jnp.einsum("oc,son->csn", own_rows, out_cot, preferred_element_type=jnp.float32),
        "chan",
        scatter_dimension=0,
        tiled=True,
    )
    onehot = (momentum[:, None] == jnp.arange(sectors, dtype=jnp.int32)[None, :]).astype(
        jnp.float32
    )
    picked = jnp.einsum("sk,akci->acsi", onehot, corr_kernels, precision=highest)
    positions = jnp.arange(lattice_side, dtype=jnp.int32)
    circ_table = (
        (positions[None, None, :] - positions[None, :, None]) % lattice_side
        == positions[:, None, None]
    ).astype(jnp.float32)
    circulant = jnp.einsum("acsi,ixy->acsxy", picked, circ_table, precision=highest)
    grid_values = input_cot.reshape(chan_block, sample_count, lattice_side, lattice_side)
    halfway = jnp.einsum("csxX,csxy->csXy", circulant[0], grid_values, precision=highest)
    corr_grad = jnp.einsum("csXy,csyY->scXY", halfway, circulant[1], precision=highest)
    corr_grad = corr_grad.reshape(sample_count, chan_block, site_count).astype(jnp.bfloat16)
    regrouped = lax.all_to_all(corr_grad, "chan", split_axis=2, concat_axis=1, tiled=True)
    spin_gate = jnp.where(spin_up == 1, 1.5, 0.5).astype(jnp.float32)[:, None, :]
    grad_now = (regrouped.astype(jnp.float32) * spin_gate).astype(jnp.bfloat16)
    halo_cells = MAXDIL * SIDE
    column = jnp.arange(slab_cells, dtype=jnp.int32) % lattice_side
    norm_factor = 1.0 / math.sqrt(sample_count * lax.axis_size("samp") * site_count)
    layer_grads = [None] * LAYERS
    input_grad = None
    for conv_level in range(LAYERS - 1, -1, -1):
        slope_base = None
        if conv_level == 0:
            layer_values = layer_input
        else:
            saved_pre = pre_one if conv_level == 1 else pre_two
            slope_base = jnp.tanh(saved_pre.astype(jnp.float32))
            layer_values = slope_base.astype(jnp.bfloat16)
        padded = with_halo(grad_now, (("chan", 2),), halo_cells)
        back_sum = jnp.zeros(grad_now.shape, jnp.float32)
        tap_grads = []
        for row_step in (-1, 0, 1):
            for col_step in (-1, 0, 1):
                tap_index = (row_step + 1) * 3 + col_step + 1
                if row_step == 0 and col_step == 0:
                    combined = grad_now
                else:
                    combined = None
                    for dilate in range(1, MAXDIL + 1):
                        slice_begin = halo_cells - row_step * dilate * lattice_side
                        shifted = column_shift(
                            padded[:, :, slice_begin : slice_begin + slab_cells],
                            col_step * dilate,
                            lattice_side,
                            column,
                        )
                        if combined is None:
                            combined = shifted
                        else:
                            chosen_mask = (dilation[conv_level] == dilate)[None, :, None]
                            combined = jnp.where(chosen_mask, shifted, combined)
                back_sum = back_sum + jnp.einsum(
                    "oc,son->scn",
                    conv_weight[conv_level, tap_index],
                    combined,
                    preferred_element_type=jnp.float32,
                )
                tap_grads.append(
                    jnp.einsum(
                        "son,scn->oc", combined, layer_values, preferred_element_type=jnp.float32
                    )
                    * norm_factor
                )
        local_grad = jnp.stack(tap_grads)
        reduced = lax.psum_scatter(
            local_grad.astype(jnp.bfloat16), "chan", scatter_dimension=1, tiled=True
        )
        layer_grads[conv_level] = lax.psum(reduced, "samp").astype(jnp.float32)
        if conv_level > 0:
            grad_now = (back_sum * (1.0 - slope_base * slope_base)).astype(jnp.bfloat16)
        else:
            input_grad = back_sum.astype(jnp.bfloat16)
    weight_grad = jnp.stack(layer_grads)
    return (input_grad, weight_grad)


def solution(mesh):
    in_specs = (
        P("samp", "chan", None),
        P(),
        P(None, None, "chan", None),
        P("samp"),
        P("samp", "chan"),
        P("samp", None, "chan"),
        P("samp", None, "chan"),
        P("samp", None, "chan"),
        P(),
        P(),
    )
    out_specs = (P("samp", None, "chan"), P(None, None, "chan", None))
    return jax.shard_map(
        on_device, mesh=mesh, in_specs=in_specs, out_specs=out_specs, check_vma=False
    )
```

profile of v0, /device:TPU:0, one launch (start us, length us, event | category | flops | bytes accessed | tf_op | source)
XLA Modules:
  0.0 344.3 jit_solution(6769106226334867354)
XLA Ops:
  7.2 3.8 %convolution_bitcast_fusion = f32[256,1,4096]{2,0,1:T(8,128)} fusion(bf16[1,64,4096]{2,1,0:T(8,128)(2,1)} %param.10, bf16[256,256]{1,0:T(8,128)(2,1)} %param.11, s32[]{:T(128)S(6)} %select_n.3285), kind=kOutput, calls=%fused_computation | convolution fusion | flops 134217728 | bytes 4751364 | tf_op jit(solution)/shard_map/oc,son->csn/dot_general | solution.py:55
  14.5 2.3 slice_bitcast_fusion
  16.8 49.8 %reduce-scatter.5.cloned.1.call-done = f32[64,1,4096]{2,0,1:T(8,128)} async-done(((f32[256,1,4096]{2,0,1:T(8,128)}), f32[64,1,4096]{2,0,1:T(8,128)}) %reduce-scatter.5.cloned.1.call-update) | async-done | bytes 1048592 | tf_op jit(solution)/shard_map/reduce_scatter | solution.py:54
  68.8 6.2 %fusion.2 = f32[64,64,64]{2,1,0:T(8,128)S(1)} fusion(f32[64,64,64]{2,1,0:T(8,128)S(1)} %reshape.16731, f32[64,64,64]{2,0,1:T(8,128)} %get-tuple-element.25), kind=kOutput, calls=%fused_computation.119 | convolution fusion | flops 201326592 | bytes 3145728 | tf_op jit(solution)/shard_map/csxX,csxy->csXy/dot_general | solution.py:71
  75.0 3.3 fusion.7
  79.2 2.8 copy.42
  82.5 23.6 %reduce.18 = bf16[4096,64]{1,0:T(8,128)(2,1)} reduce(bf16[4096,1,64]{2,1,0:T(2,128)(2,1)S(1)} %bitcast.976, bf16[]{:T(256)} %broadcast.4323), dimensions={1}, to_apply=%bitcast.918.reduce_sub_computation | reduce | bytes 1048578
  106.1 2.7 reshape.16776
  108.7 3.5 %all-to-all-start = ((bf16[4,2,32768]{2,1,0:T(2,128)(2,1)}), bf16[4,2,32768]{2,1,0:T(2,128)(2,1)S(1)}, u32[]{:S(2)}, u32[]{:S(2)}) async-start(bf16[4,2,32768]{2,1,0:T(2,128)(2,1)} %reshape.16776), calls=%async_computation.1 | async-start | bytes 1048576 | tf_op jit(solution)/shard_map/all_to_all | solution.py:74
  114.4 6.1 %all-to-all-done = bf16[4,2,32768]{2,1,0:T(2,128)(2,1)S(1)} async-done(((bf16[4,2,32768]{2,1,0:T(2,128)(2,1)}), bf16[4,2,32768]{2,1,0:T(2,128)(2,1)S(1)}, u32[]{:S(2)}, u32[]{:S(2)}) %all-to-all-start) | async-done | bytes 524320 | tf_op jit(solution)/shard_map/all_to_all | solution.py:74
  129.6 4.8 %collective-permute-done = bf16[1,256,256]{1,2,0:T(8,128)(2,1)S(1)} collective-permute-done((bf16[1,256,256]{1,2,0:T(8,128)(2,1)S(1)}, bf16[1,256,256]{1,2,0:T(8,128)(2,1)S(1)}, u32[]{:S(2)}, u32[]{:S(2)}) %collective-permute-start) | collective-permute-done | bytes 131104 | tf_op jit(solution)/shard_map/ppermute | solution.py:20
  137.4 3.0 fusion.252
  143.4 3.0 fusion.256
  147.6 3.0 fusion.260
  153.1 3.0 fusion.264
  157.4 3.0 fusion.268
  162.9 3.0 fusion.272
  177.7 3.0 fusion.276
  183.7 3.0 fusion.280
  187.9 3.0 fusion.284
  193.4 3.0 fusion.288
  197.6 3.0 fusion.292
  203.1 3.0 fusion.296
  218.1 3.0 fusion.300
  223.8 3.0 fusion.304
  227.8 3.0 fusion.308
  232.9 3.0 fusion.312
  236.8 3.0 fusion.316
  241.9 3.0 fusion.320
  254.7 20.1 %reduce-scatter.7.cloned.1.call-done = bf16[9,64,256]{2,1,0:T(8,128)(2,1)} async-done(((bf16[9,256,256]{2,1,0:T(8,128)(2,1)}), bf16[9,64,256]{2,1,0:T(8,128)(2,1)}) %reduce-scatter.7.cloned.1.call-update) | async-done | bytes 294928 | tf_op jit(solution)/shard_map/reduce_scatter | solution.py:126
  278.4 56.7 %all-reduce.3.cloned.1.call-done = (bf16[1,9,64,256]{3,2,1,0:T(8,128)(2,1)}, bf16[1,9,64,256]{3,2,1,0:T(8,128)(2,1)}, bf16[1,9,64,256]{3,2,1,0:T(8,128)(2,1)}) async-done(((bf16[1,9,64,256]{3,2,1,0:T(8,128)(2,1)}, bf16[1,9,64,256]{3,2,1,0:T(8,128)(2,1)}, bf16[1,9,64,256]{3,2,1,0:T(8,128)(2,1)}), (bf16[1,9,64,256]{3,2,1,0:T(8,128)(2,1)}, bf16[1,9,64,256]{3,2,1,0:T(8,128)(2,1)}, ...) | async-done | bytes 884752 | tf_op jit(solution)/shard_map/psum | solution.py:129
  335.0 2.5 maximum_convert_fusion
  (242 shorter events, 86.0 us)
Async XLA Ops:
  7.2 4.7 %copy-start = (f32[2,12,64,64]{3,2,1,0:T(8,128)S(1)}, f32[2,12,64,64]{3,2,1,0:T(8,128)}, u32[]{:S(2)}) copy-start(f32[2,12,64,64]{3,2,1,0:T(8,128)} %param.12) | copy-start | bytes 1179652
  7.2 59.5 %reduce-scatter.5.cloned.1.call-start = ((), (), s32[]{:S(2)}) async-start(), calls=%async_computation.5 | async-start | bytes 5242880 | tf_op jit(solution)/shard_map/reduce_scatter | solution.py:54
  68.8 6.2 %copy-start.2 = (f32[64,64,64]{2,0,1:T(8,128)S(1)}, f32[64,64,64]{2,0,1:T(8,128)}, u32[]{:S(2)}) copy-start(f32[64,64,64]{2,0,1:T(8,128)} %get-tuple-element.24) | copy-start | bytes 3145732
  106.1 6.2 %copy-start.15 = (bf16[1,256,1024]{2,1,0:T(8,128)(2,1)S(1)}, bf16[1,256,1024]{2,1,0:T(8,128)(2,1)}, u32[]{:S(2)}) copy-start(bf16[1,256,1024]{2,1,0:T(8,128)(2,1)} %param.16) | copy-start | bytes 1572868
  106.1 7.2 %copy-start.16 = (bf16[1,256,1024]{2,1,0:T(8,128)(2,1)S(1)}, bf16[1,256,1024]{2,1,0:T(8,128)(2,1)}, u32[]{:S(2)}) copy-start(bf16[1,256,1024]{2,1,0:T(8,128)(2,1)} %param.17) | copy-start | bytes 1572868
  106.1 8.2 %copy-start.18 = (s32[3,256]{1,0:T(4,128)S(1)}, s32[3,256]{1,0:T(4,128)}, u32[]{:S(2)}) copy-start(s32[3,256]{1,0:T(4,128)} %param.19) | copy-start | bytes 9220
  106.1 8.3 %copy-start.17 = (s32[1,1024]{1,0:T(1,128)S(1)}, s32[1,1024]{1,0:T(1,128)}, u32[]{:S(2)}) copy-start(s32[1,1024]{1,0:T(1,128)} %param.14) | copy-start | bytes 12292
  108.7 11.7 %all-to-all-start = ((bf16[4,2,32768]{2,1,0:T(2,128)(2,1)}), bf16[4,2,32768]{2,1,0:T(2,128)(2,1)S(1)}, u32[]{:S(2)}, u32[]{:S(2)}) async-start(bf16[4,2,32768]{2,1,0:T(2,128)(2,1)} %reshape.16776), calls=%async_computation.1 | async-start | bytes 1048576 | tf_op jit(solution)/shard_map/all_to_all | solution.py:74
  112.2 142.5 %reduce-scatter.11.cloned.1.call-start = ((), (), s32[]{:S(2)}) async-start(), calls=%async_computation.8 | async-start | bytes 1474560 | tf_op jit(solution)/shard_map/reduce_scatter | solution.py:126
  126.2 8.3 %collective-permute-start.1 = (bf16[1,256,256]{1,2,0:T(8,128)(2,1)S(1)}, bf16[1,256,256]{1,2,0:T(8,128)(2,1)S(1)}, u32[]{:S(2)}, u32[]{:S(2)}) collective-permute-start(bf16[1,256,256]{1,2,0:T(8,128)(2,1)S(1)} %get-tuple-element.324), channel_id=1, source_target_pairs={{0,1},{1,2},{2,3},{3,0},{4,5},{5,6},{6,7},{7,4},{8,9},{9,10},{10,1... | collective-permute-start | bytes 393224 | tf_op jit(solution)/shard_map/ppermute | solution.py:19
  127.7 6.7 %collective-permute-start = (bf16[1,256,256]{1,2,0:T(8,128)(2,1)S(1)}, bf16[1,256,256]{1,2,0:T(8,128)(2,1)S(1)}, u32[]{:S(2)}, u32[]{:S(2)}) collective-permute-start(bf16[1,256,256]{1,2,0:T(8,128)(2,1)S(1)} %get-tuple-element.325), channel_id=1, source_target_pairs={{1,0},{2,1},{3,2},{0,3},{5,4},{6,5},{7,6},{4,7},{9,8},{10,9},{11,1... | collective-permute-start | bytes 393224 | tf_op jit(solution)/shard_map/ppermute | solution.py:20
  162.9 3.0 copy-start.8
  167.7 7.3 %collective-permute-start.3 = (bf16[1,256,256]{1,2,0:T(8,128)(2,1)S(1)}, bf16[1,256,256]{1,2,0:T(8,128)(2,1)S(1)}, u32[]{:S(2)}, u32[]{:S(2)}) collective-permute-start(bf16[1,256,256]{1,2,0:T(8,128)(2,1)S(1)} %get-tuple-element.258), channel_id=1, source_target_pairs={{0,1},{1,2},{2,3},{3,0},{4,5},{5,6},{6,7},{7,4},{8,9},{9,10},{10,1... | collective-permute-start | bytes 393224 | tf_op jit(solution)/shard_map/ppermute | solution.py:19
  168.8 6.1 %collective-permute-start.2 = (bf16[1,256,256]{1,2,0:T(8,128)(2,1)S(1)}, bf16[1,256,256]{1,2,0:T(8,128)(2,1)S(1)}, u32[]{:S(2)}, u32[]{:S(2)}) collective-permute-start(bf16[1,256,256]{1,2,0:T(8,128)(2,1)S(1)} %get-tuple-element.259), channel_id=1, source_target_pairs={{1,0},{2,1},{3,2},{0,3},{5,4},{6,5},{7,6},{4,7},{9,8},{10,9},{11,1... | collective-permute-start | bytes 393224 | tf_op jit(solution)/shard_map/ppermute | solution.py:20
  173.8 1.0 copy-start.13
  174.8 79.9 %reduce-scatter.9.cloned.1.call-start = ((), (), s32[]{:S(2)}) async-start(), calls=%async_computation.7 | async-start | bytes 1474560 | tf_op jit(solution)/shard_map/reduce_scatter | solution.py:126
  203.1 3.0 copy-start.7
  207.6 7.8 %collective-permute-start.5 = (bf16[1,256,256]{1,2,0:T(8,128)(2,1)S(1)}, bf16[1,256,256]{1,2,0:T(8,128)(2,1)S(1)}, u32[]{:S(2)}, u32[]{:S(2)}) collective-permute-start(bf16[1,256,256]{1,2,0:T(8,128)(2,1)S(1)} %get-tuple-element.192), channel_id=1, source_target_pairs={{0,1},{1,2},{2,3},{3,0},{4,5},{5,6},{6,7},{7,4},{8,9},{9,10},{10,1... | collective-permute-start | bytes 393224 | tf_op jit(solution)/shard_map/ppermute | solution.py:19
  208.5 6.8 %collective-permute-start.4 = (bf16[1,256,256]{1,2,0:T(8,128)(2,1)S(1)}, bf16[1,256,256]{1,2,0:T(8,128)(2,1)S(1)}, u32[]{:S(2)}, u32[]{:S(2)}) collective-permute-start(bf16[1,256,256]{1,2,0:T(8,128)(2,1)S(1)} %get-tuple-element.193), channel_id=1, source_target_pairs={{1,0},{2,1},{3,2},{0,3},{5,4},{6,5},{7,6},{4,7},{9,8},{10,9},{11,1... | collective-permute-start | bytes 393224 | tf_op jit(solution)/shard_map/ppermute | solution.py:20
  213.9 1.0 copy-start.14
  215.0 59.8 %reduce-scatter.7.cloned.1.call-start = ((), (), s32[]{:S(2)}) async-start(), calls=%async_computation.6 | async-start | bytes 1474560 | tf_op jit(solution)/shard_map/reduce_scatter | solution.py:126
  218.1 3.0 copy-start.19
  222.7 4.1 %copy-start.11 = (bf16[256,1024]{0,1:T(8,128)(2,1)}, bf16[256,1024]{0,1:T(8,128)(2,1)S(1)}, u32[]{:S(2)}) copy-start(bf16[256,1024]{0,1:T(8,128)(2,1)S(1)} %get-tuple-element.123) | copy-start | bytes 1572868
  222.7 18.2 %copy-start.9 = (bf16[256,1024]{0,1:T(8,128)(2,1)}, bf16[256,1024]{0,1:T(8,128)(2,1)S(1)}, u32[]{:S(2)}) copy-start(bf16[256,1024]{0,1:T(8,128)(2,1)S(1)} %get-tuple-element.122) | copy-start | bytes 1572868
  235.8 4.0 %copy-start.3 = (bf16[256,1024]{0,1:T(8,128)(2,1)}, bf16[256,1024]{0,1:T(8,128)(2,1)S(1)}, u32[]{:S(2)}) copy-start(bf16[256,1024]{0,1:T(8,128)(2,1)S(1)} %fusion.312) | copy-start | bytes 1572868
  239.8 2.0 copy-start.5
  244.8 2.3 copy-start.12
  245.9 89.1 %all-reduce.3.cloned.1.call-start = ((), (), s32[]{:S(2)}) async-start(), calls=%async_computation.9 | async-start | bytes 1769472 | tf_op jit(solution)/shard_map/psum | solution.py:129
  249.6 2.6 copy-start.4
  250.8 2.5 copy-start.6
  253.4 21.5 %copy-start.10 = (bf16[256,1024]{0,1:T(8,128)(2,1)S(1)}, bf16[256,1024]{0,1:T(8,128)(2,1)}, u32[]{:S(2)}) copy-start(bf16[256,1024]{0,1:T(8,128)(2,1)} %copy-done.9) | copy-start | bytes 1572868
  276.1 61.5 %copy-start.1 = (f32[2,12,64,64]{3,2,1,0:T(8,128)S(1)}, f32[2,12,64,64]{3,2,1,0:T(8,128)}, u32[]{:S(2)}) copy-start(f32[2,12,64,64]{3,2,1,0:T(8,128)} %param.12) | copy-start | bytes 1179652
Sparse Core Ops, SparseCore 0:
  11.2 55.3 reduce-scatter.4
  174.9 27.8 reduce-scatter.10
  215.1 28.0 reduce-scatter.8
  246.3 28.5 reduce-scatter.6
  277.4 57.5 all-reduce.2
where the time goes:
time: 348 us; the launch traced here: 344 us
  waiting for transfers between devices  138 us (40%)
  other arithmetic  90.3 us (26%)
  matrix products  64.6 us (19%)
  local copies, waits for them, and re-layouts  22.2 us (6%)
  between operations  16.2 us (5%)
  starting transfers between devices  13.4 us (4%)
    psum x1, waiting for transfers between devices, on_device(): layer_grads[conv_level] = lax.psum(reduced, 'samp').astype(jnp.float32)  56.7 us
    select_n x18, other arithmetic, on_device(): combined = jnp.where(chosen_mask, shifted, combined)  54 us
    reduce_scatter x1, waiting for transfers between devices, on_device(): lax.psum_scatter(jnp.einsum('oc,son->csn', own_rows, out_cot, preferred_e...  49.8 us
    dot_general x27, matrix products, on_device(): jnp.einsum('oc,son->scn', conv_weight[conv_level, tap_index], combined, p...  32.9 us
    unnamed x1, other arithmetic  23.6 us
    reduce_scatter x3, waiting for transfers between devices, on_device(): lax.psum_scatter(local_grad.astype(jnp.bfloat16), 'chan', scatter_dimensi...  20.1 us
    dot_general x27, matrix products, on_device(): jnp.einsum('son,scn->oc', combined, layer_values, preferred_element_type=...  15.7 us
    unnamed x46, local copies, waits for them, and re-layouts  9.22 us
  transfers between devices with their start and end apart: 12, of which 5 were waited for; matrix products, arithmetic and copies ran while one was open for 26% of the time, Pallas kernels for 0%

commit v1 on v0

--- a/solution.py
+++ b/solution.py
@@ -7,6 +7,12 @@
 SIDE = 64
 LAYERS = 3
 MAXDIL = 4
+
+
+def gather_and_add(array, axis):
+    pieces = lax.all_gather(array, axis, axis=0, tiled=False)
+    total = pieces.sum(axis=0)
+    return total
 
 
 def with_halo(shard, sides, width):
@@ -126,7 +132,7 @@
         reduced = lax.psum_scatter(
             local_grad.astype(jnp.bfloat16), "chan", scatter_dimension=1, tiled=True
         )
-        layer_grads[conv_level] = lax.psum(reduced, "samp").astype(jnp.float32)
+        layer_grads[conv_level] = gather_and_add(reduced, "samp").astype(jnp.float32)
         if conv_level > 0:
             grad_now = (back_sum * (1.0 - slope_base * slope_base)).astype(jnp.bfloat16)
         else:

time: 348 us -> 388 us (1.11)
  waiting for transfers between devices: 138 us -> 171 us
  other arithmetic: 90.3 us -> 95.5 us
    all_gather x0 -> x3, waiting for transfers between devices: none -> 81.6 us  [gather_and_add(): pieces = lax.all_gather(array, axis, axis=0, tiled=False)]
    psum x1 -> x0, waiting for transfers between devices: 56.7 us -> none  [on_device(): layer_grads[conv_level] = lax.psum(reduced, 'samp').astype(jnp.float32)]
    reduce_scatter x3, waiting for transfers between devices: 20.1 us -> 27.7 us  [on_device(): lax.psum_scatter(local_grad.astype(jnp.bfloat16), 'chan', scatter_dimensi...]
    reduce_sum x0 -> x3, other arithmetic: none -> 6.4 us  [gather_and_add(): total = pieces.sum(axis=0)]
    unnamed x46 -> x40, local copies, waits for them, and re-layouts: 9.22 us -> 9.21 us
  transfers between devices with their start and end apart: 12 -> 14, of which waited for: 5 -> 7; matrix products, arithmetic and copies ran while one was open for 26% -> 24% of each run, Pallas kernels for 0% -> 0%
where the time goes in v1:
time: 388 us; the launch traced here: 384 us
  waiting for transfers between devices  171 us (44%)
  other arithmetic  95.5 us (25%)
  matrix products  64.6 us (17%)
  local copies, waits for them, and re-layouts  22.2 us (6%)
  between operations  16.6 us (4%)
  starting transfers between devices  13.7 us (4%)
    all_gather x3, waiting for transfers between devices, gather_and_add(): pieces = lax.all_gather(array, axis, axis=0, tiled=False)  81.6 us
    select_n x18, other arithmetic, on_device(): combined = jnp.where(chosen_mask, shifted, combined)  54 us
    reduce_scatter x1, waiting for transfers between devices, on_device(): lax.psum_scatter(jnp.einsum('oc,son->csn', own_rows, out_cot, preferred_e...  49.8 us
    dot_general x27, matrix products, on_device(): jnp.einsum('oc,son->scn', conv_weight[conv_level, tap_index], combined, p...  32.9 us
    reduce_scatter x3, waiting for transfers between devices, on_device(): lax.psum_scatter(local_grad.astype(jnp.bfloat16), 'chan', scatter_dimensi...  27.7 us
    unnamed x1, other arithmetic  23.6 us
    dot_general x27, matrix products, on_device(): jnp.einsum('son,scn->oc', combined, layer_values, preferred_element_type=...  15.7 us
    unnamed x40, local copies, waits for them, and re-layouts  9.21 us
  transfers between devices with their start and end apart: 14, of which 7 were waited for; matrix products, arithmetic and copies ran while one was open for 24% of the time, Pallas kernels for 0%

profile of v1, /device:TPU:0, one launch (start us, length us, event | category | flops | bytes accessed | tf_op | source)
XLA Modules:
  0.0 383.7 jit_solution(12662061163557476276)
XLA Ops:
  7.2 3.8 convolution_bitcast_fusion
  16.8 49.8 %reduce-scatter.5.cloned.1.call-done = f32[64,1,4096]{2,0,1:T(8,128)} async-done(((f32[256,1,4096]{2,0,1:T(8,128)}), f32[64,1,4096]{2,0,1:T(8,128)}) %reduce-scatter.5.cloned.1.call-update) | async-done | bytes 1048592 | tf_op jit(solution)/shard_map/reduce_scatter | solution.py:60
  68.8 6.2 %fusion.2 = f32[64,64,64]{2,1,0:T(8,128)S(1)} fusion(f32[64,64,64]{2,1,0:T(8,128)S(1)} %reshape.16758, f32[64,64,64]{2,0,1:T(8,128)} %get-tuple-element.22), kind=kOutput, calls=%fused_computation.119 | convolution fusion | flops 201326592 | bytes 3145728 | tf_op jit(solution)/shard_map/csxX,csxy->csXy/dot_general | solution.py:77
  75.0 3.3 fusion.7
  79.1 2.8 copy.42
  82.4 23.6 %reduce.21 = bf16[4096,64]{1,0:T(8,128)(2,1)} reduce(bf16[4096,1,64]{2,1,0:T(2,128)(2,1)S(1)} %bitcast.979, bf16[]{:T(256)} %broadcast.4323), dimensions={1}, to_apply=%bitcast.921.reduce_sub_computation | reduce | bytes 1048578
  106.0 2.7 reshape.16806
  108.7 3.5 all-to-all-start
  114.3 6.1 %all-to-all-done = bf16[4,2,32768]{2,1,0:T(2,128)(2,1)S(1)} async-done(((bf16[4,2,32768]{2,1,0:T(2,128)(2,1)}), bf16[4,2,32768]{2,1,0:T(2,128)(2,1)S(1)}, u32[]{:S(2)}, u32[]{:S(2)}) %all-to-all-start) | async-done | bytes 524320 | tf_op jit(solution)/shard_map/all_to_all | solution.py:80
  129.6 4.8 %collective-permute-done = bf16[1,256,256]{1,2,0:T(8,128)(2,1)S(1)} collective-permute-done((bf16[1,256,256]{1,2,0:T(8,128)(2,1)S(1)}, bf16[1,256,256]{1,2,0:T(8,128)(2,1)S(1)}, u32[]{:S(2)}, u32[]{:S(2)}) %collective-permute-start) | collective-permute-done | bytes 131104 | tf_op jit(solution)/shard_map/ppermute | solution.py:26
  137.4 3.0 fusion.252
  143.4 3.0 fusion.256
  147.6 3.0 fusion.260
  153.1 3.0 fusion.264
  157.4 3.0 fusion.268
  162.9 3.0 fusion.272
  177.8 3.0 fusion.276
  183.8 3.0 fusion.280
  188.0 3.0 fusion.284
  193.5 3.0 fusion.288
  197.7 3.0 fusion.292
  203.2 3.0 fusion.296
  218.2 3.0 fusion.300
  223.8 3.0 fusion.304
  227.8 3.0 fusion.308
  232.9 3.0 fusion.312
  236.9 3.0 fusion.316
  241.9 3.0 fusion.320
  247.3 27.7 %reduce-scatter.7.cloned.1.call-done = bf16[9,64,256]{2,1,0:T(8,128)(2,1)} async-done(((bf16[9,256,256]{2,1,0:T(8,128)(2,1)}), bf16[9,64,256]{2,1,0:T(8,128)(2,1)}) %reduce-scatter.7.cloned.1.call-update) | async-done | bytes 294928 | tf_op jit(solution)/shard_map/reduce_scatter | solution.py:132
  287.2 21.0 %all-gather.11.cloned.1.call-done = bf16[72,64,256]{2,1,0:T(8,128)(2,1)} async-done(((bf16[9,64,256]{2,1,0:T(8,128)(2,1)}), bf16[72,64,256]{2,1,0:T(8,128)(2,1)}) %all-gather.11.cloned.1.call-update) | async-done | bytes 2359312 | tf_op jit(solution)/shard_map/all_gather | solution.py:13
  310.3 30.2 %all-gather.9.cloned.1.call-done = bf16[72,64,256]{2,1,0:T(8,128)(2,1)} async-done(((bf16[9,64,256]{2,1,0:T(8,128)(2,1)}), bf16[72,64,256]{2,1,0:T(8,128)(2,1)}) %all-gather.9.cloned.1.call-update) | async-done | bytes 2359312 | tf_op jit(solution)/shard_map/all_gather | solution.py:13
  342.7 30.4 %all-gather.7.cloned.1.call-done = bf16[72,64,256]{2,1,0:T(8,128)(2,1)} async-done(((bf16[9,64,256]{2,1,0:T(8,128)(2,1)}), bf16[72,64,256]{2,1,0:T(8,128)(2,1)}) %all-gather.7.cloned.1.call-update) | async-done | bytes 2359312 | tf_op jit(solution)/shard_map/all_gather | solution.py:13
  (245 shorter events, 97.3 us)
Async XLA Ops:
  7.2 4.6 %copy-start = (f32[2,12,64,64]{3,2,1,0:T(8,128)S(1)}, f32[2,12,64,64]{3,2,1,0:T(8,128)}, u32[]{:S(2)}) copy-start(f32[2,12,64,64]{3,2,1,0:T(8,128)} %param.12) | copy-start | bytes 1179652
  7.2 59.5 %reduce-scatter.5.cloned.1.call-start = ((), (), s32[]{:S(2)}) async-start(), calls=%async_computation.5 | async-start | bytes 5242880 | tf_op jit(solution)/shard_map/reduce_scatter | solution.py:60
  68.8 6.2 %copy-start.2 = (f32[64,64,64]{2,0,1:T(8,128)S(1)}, f32[64,64,64]{2,0,1:T(8,128)}, u32[]{:S(2)}) copy-start(f32[64,64,64]{2,0,1:T(8,128)} %get-tuple-element.21) | copy-start | bytes 3145732
  106.0 6.2 %copy-start.12 = (bf16[1,256,1024]{2,1,0:T(8,128)(2,1)S(1)}, bf16[1,256,1024]{2,1,0:T(8,128)(2,1)}, u32[]{:S(2)}) copy-start(bf16[1,256,1024]{2,1,0:T(8,128)(2,1)} %param.16) | copy-start | bytes 1572868
  106.0 7.2 %copy-start.13 = (bf16[1,256,1024]{2,1,0:T(8,128)(2,1)S(1)}, bf16[1,256,1024]{2,1,0:T(8,128)(2,1)}, u32[]{:S(2)}) copy-start(bf16[1,256,1024]{2,1,0:T(8,128)(2,1)} %param.17) | copy-start | bytes 1572868
  106.0 8.2 %copy-start.15 = (s32[3,256]{1,0:T(4,128)S(1)}, s32[3,256]{1,0:T(4,128)}, u32[]{:S(2)}) copy-start(s32[3,256]{1,0:T(4,128)} %param.19) | copy-start | bytes 9220
  106.0 8.3 %copy-start.14 = (s32[1,1024]{1,0:T(1,128)S(1)}, s32[1,1024]{1,0:T(1,128)}, u32[]{:S(2)}) copy-start(s32[1,1024]{1,0:T(1,128)} %param.14) | copy-start | bytes 12292
  108.7 11.7 %all-to-all-start = ((bf16[4,2,32768]{2,1,0:T(2,128)(2,1)}), bf16[4,2,32768]{2,1,0:T(2,128)(2,1)S(1)}, u32[]{:S(2)}, u32[]{:S(2)}) async-start(bf16[4,2,32768]{2,1,0:T(2,128)(2,1)} %reshape.16806), calls=%async_computation.1 | async-start | bytes 1048576 | tf_op jit(solution)/shard_map/all_to_all | solution.py:80
  112.2 133.7 %reduce-scatter.11.cloned.1.call-start = ((), (), s32[]{:S(2)}) async-start(), calls=%async_computation.8 | async-start | bytes 1474560 | tf_op jit(solution)/shard_map/reduce_scatter | solution.py:132
  126.2 8.3 %collective-permute-start.1 = (bf16[1,256,256]{1,2,0:T(8,128)(2,1)S(1)}, bf16[1,256,256]{1,2,0:T(8,128)(2,1)S(1)}, u32[]{:S(2)}, u32[]{:S(2)}) collective-permute-start(bf16[1,256,256]{1,2,0:T(8,128)(2,1)S(1)} %get-tuple-element.321), channel_id=1, source_target_pairs={{0,1},{1,2},{2,3},{3,0},{4,5},{5,6},{6,7},{7,4},{8,9},{9,10},{10,1... | collective-permute-start | bytes 393224 | tf_op jit(solution)/shard_map/ppermute | solution.py:25
  127.7 6.7 %collective-permute-start = (bf16[1,256,256]{1,2,0:T(8,128)(2,1)S(1)}, bf16[1,256,256]{1,2,0:T(8,128)(2,1)S(1)}, u32[]{:S(2)}, u32[]{:S(2)}) collective-permute-start(bf16[1,256,256]{1,2,0:T(8,128)(2,1)S(1)} %get-tuple-element.322), channel_id=1, source_target_pairs={{1,0},{2,1},{3,2},{0,3},{5,4},{6,5},{7,6},{4,7},{9,8},{10,9},{11,1... | collective-permute-start | bytes 393224 | tf_op jit(solution)/shard_map/ppermute | solution.py:26
  162.9 3.0 copy-start.6
  167.7 7.3 %collective-permute-start.3 = (bf16[1,256,256]{1,2,0:T(8,128)(2,1)S(1)}, bf16[1,256,256]{1,2,0:T(8,128)(2,1)S(1)}, u32[]{:S(2)}, u32[]{:S(2)}) collective-permute-start(bf16[1,256,256]{1,2,0:T(8,128)(2,1)S(1)} %get-tuple-element.255), channel_id=1, source_target_pairs={{0,1},{1,2},{2,3},{3,0},{4,5},{5,6},{6,7},{7,4},{8,9},{9,10},{10,1... | collective-permute-start | bytes 393224 | tf_op jit(solution)/shard_map/ppermute | solution.py:25
  168.9 6.1 %collective-permute-start.2 = (bf16[1,256,256]{1,2,0:T(8,128)(2,1)S(1)}, bf16[1,256,256]{1,2,0:T(8,128)(2,1)S(1)}, u32[]{:S(2)}, u32[]{:S(2)}) collective-permute-start(bf16[1,256,256]{1,2,0:T(8,128)(2,1)S(1)} %get-tuple-element.256), channel_id=1, source_target_pairs={{1,0},{2,1},{3,2},{0,3},{5,4},{6,5},{7,6},{4,7},{9,8},{10,9},{11,1... | collective-permute-start | bytes 393224 | tf_op jit(solution)/shard_map/ppermute | solution.py:26
  173.8 1.0 copy-start.10
  174.9 71.6 %reduce-scatter.9.cloned.1.call-start = ((), (), s32[]{:S(2)}) async-start(), calls=%async_computation.7 | async-start | bytes 1474560 | tf_op jit(solution)/shard_map/reduce_scatter | solution.py:132
  203.2 3.0 copy-start.5
  207.7 7.8 %collective-permute-start.5 = (bf16[1,256,256]{1,2,0:T(8,128)(2,1)S(1)}, bf16[1,256,256]{1,2,0:T(8,128)(2,1)S(1)}, u32[]{:S(2)}, u32[]{:S(2)}) collective-permute-start(bf16[1,256,256]{1,2,0:T(8,128)(2,1)S(1)} %get-tuple-element.189), channel_id=1, source_target_pairs={{0,1},{1,2},{2,3},{3,0},{4,5},{5,6},{6,7},{7,4},{8,9},{9,10},{10,1... | collective-permute-start | bytes 393224 | tf_op jit(solution)/shard_map/ppermute | solution.py:25
  208.6 6.8 %collective-permute-start.4 = (bf16[1,256,256]{1,2,0:T(8,128)(2,1)S(1)}, bf16[1,256,256]{1,2,0:T(8,128)(2,1)S(1)}, u32[]{:S(2)}, u32[]{:S(2)}) collective-permute-start(bf16[1,256,256]{1,2,0:T(8,128)(2,1)S(1)} %get-tuple-element.190), channel_id=1, source_target_pairs={{1,0},{2,1},{3,2},{0,3},{5,4},{6,5},{7,6},{4,7},{9,8},{10,9},{11,1... | collective-permute-start | bytes 393224 | tf_op jit(solution)/shard_map/ppermute | solution.py:26
  214.2 1.1 copy-start.11
  215.3 59.7 %reduce-scatter.7.cloned.1.call-start = ((), (), s32[]{:S(2)}) async-start(), calls=%async_computation.6 | async-start | bytes 1474560 | tf_op jit(solution)/shard_map/reduce_scatter | solution.py:132
  218.2 3.0 copy-start.16
  222.7 4.1 %copy-start.9 = (bf16[256,1024]{0,1:T(8,128)(2,1)}, bf16[256,1024]{0,1:T(8,128)(2,1)S(1)}, u32[]{:S(2)}) copy-start(bf16[256,1024]{0,1:T(8,128)(2,1)S(1)} %get-tuple-element.120) | copy-start | bytes 1572868
  222.7 18.1 %copy-start.7 = (bf16[256,1024]{0,1:T(8,128)(2,1)}, bf16[256,1024]{0,1:T(8,128)(2,1)S(1)}, u32[]{:S(2)}) copy-start(bf16[256,1024]{0,1:T(8,128)(2,1)S(1)} %get-tuple-element.119) | copy-start | bytes 1572868
  239.9 2.0 copy-start.3
  245.9 62.4 %all-gather.11.cloned.1.call-start = ((), (), s32[]{:S(2)}) async-start(), calls=%async_computation.11 | async-start | bytes 2654208 | tf_op jit(solution)/shard_map/all_gather | solution.py:13
  246.4 94.1 %all-gather.9.cloned.1.call-start = ((), (), s32[]{:S(2)}) async-start(), calls=%async_computation.10 | async-start | bytes 2654208 | tf_op jit(solution)/shard_map/all_gather | solution.py:13
  247.0 126.1 %all-gather.7.cloned.1.call-start = ((), (), s32[]{:S(2)}) async-start(), calls=%async_computation.9 | async-start | bytes 2654208 | tf_op jit(solution)/shard_map/all_gather | solution.py:13
  280.0 2.6 copy-start.4
  281.3 2.5 copy-start.8
  373.1 3.5 copy-start.1
Sparse Core Ops, SparseCore 0:
  11.2 55.3 reduce-scatter.4
  175.0 27.7 reduce-scatter.10
  215.4 27.9 reduce-scatter.8
  246.4 28.5 reduce-scatter.6
  276.6 31.5 all-gather.10
  309.8 30.7 all-gather.8
  342.3 30.7 all-gather.6
